TPU v7x, 32 devices: a whole 2x2x4 slice. The times are simulated.
32 devices in a mesh: rows: 8 (over z, x), heads: 4 (over y, core).
Axes of the slice: x: 2, y: 2, z: 4, core: 2. Of those that a mesh axis runs over, the one named last changes fastest.
Arguments:
- patches: float32 [16384, 48], P(('rows', 'heads')), may hold values from -6 to 6
- segments: int32 [16384], P('rows'), may hold values from 0 to 3, as said below
- labels: int32 [64, 4], P(('rows', 'heads')), may hold values from 0 to 999
- w_in: bfloat16 [48, 768], replicated, may hold values from -0.875 to 0.875
- b_in: float32 [768], replicated, may hold values from -3 to 3
- pos_table: bfloat16 [256, 768], replicated, may hold values from -3 to 3
- cls_table: bfloat16 [1000, 768], replicated, may hold values from -3 to 3
- ln1_gain: float32 [1, 768], replicated, may hold values from 0.1 to 1.9
- ln1_bias: float32 [1, 768], replicated, may hold values from -2 to 2
- w_query: bfloat16 [1, 768, 768], P(None, None, 'heads'), may hold values from -0.21875 to 0.21875
- w_key: bfloat16 [1, 768, 768], P(None, None, 'heads'), may hold values from -0.21875 to 0.21875
- w_value: bfloat16 [1, 768, 768], P(None, None, 'heads'), may hold values from -0.21875 to 0.21875
- w_attn_out: bfloat16 [1, 768, 768], P(None, 'heads'), may hold values from -1.25 to 1.25
- ln2_gain: float32 [1, 768], replicated, may hold values from 0.1 to 1.9
- ln2_bias: float32 [1, 768], replicated, may hold values from -2 to 2
- w_up: bfloat16 [1, 768, 3072], P(None, None, 'heads'), may hold values from -0.21875 to 0.21875
- b_up: bfloat16 [1, 3072], P(None, 'heads'), may hold values from -3 to 3
- w_down: bfloat16 [1, 3072, 768], P(None, 'heads'), may hold values from -0.109375 to 0.109375
- b_down: float32 [1, 768], replicated, may hold values from -3 to 3
- w_out: bfloat16 [768, 96], replicated, may hold values from -0.02734375 to 0.02734375
- b_out: float32 [96], replicated, may hold values from -2 to 2
- latent_grad: float32 [16384, 48], P(('rows', 'heads')), may hold values from -6 to 6
- logdet_grad: float32 [16384], P(('rows', 'heads')), may hold values from -6 to 6
Outputs:
- latents: float32 [16384, 48], P(('rows', 'heads'))
- logdet: float32 [16384], P(('rows', 'heads'))
- patches_grad: float32 [16384, 48], P(('rows', 'heads'))
- scale_mean: float32 [64], P(('rows', 'heads'))
- scale_max: float32 [64], P(('rows', 'heads'))
- w_in_grad: float32 [48, 768], replicated
- b_in_grad: float32 [768], replicated
- pos_table_grad: float32 [256, 768], replicated
- cls_table_grad: float32 [1000, 768], replicated
- ln1_gain_grad: float32 [1, 768], replicated
- ln1_bias_grad: float32 [1, 768], replicated
- w_query_grad: float32 [1, 768, 768], P(None, None, 'heads')
- w_key_grad: float32 [1, 768, 768], P(None, None, 'heads')
- w_value_grad: float32 [1, 768, 768], P(None, None, 'heads')
- w_attn_out_grad: float32 [1, 768, 768], P(None, 'heads')
- ln2_gain_grad: float32 [1, 768], replicated
- ln2_bias_grad: float32 [1, 768], replicated
- w_up_grad: float32 [1, 768, 3072], P(None, None, 'heads')
- b_up_grad: float32 [1, 3072], P(None, 'heads')
- w_down_grad: float32 [1, 3072, 768], P(None, 'heads')
- b_down_grad: float32 [1, 768], replicated
- w_out_grad: float32 [768, 96], replicated
- b_out_grad: float32 [96], replicated
Inputs may be any that keep to these rules, and one draw needn't show every extreme that they name: Each row of 256 patches is either one segment numbered 0, or 4 segments of 64 patches numbered 0 to 3 in order; the first row is of the second kind.
All inputs are finite; a program needn't handle non-finite values.
Results may differ from a plain program's by a relative error of at most 0.034.
Values may be sent and summed in bfloat16 or wider, within the bound.
No kernel may reach another device: no remote copies, remote signals or barrier semaphores. Data moves between devices by JAX's collectives and lax.ppermute only.
A program may use at most 128 MiB of HBM per device.

v0:
```python
import jax
import jax.numpy as jnp
from jax import lax
from jax.sharding import PartitionSpec as P

HEAD_DIM = 64
EPSILON = 1e-05
PRECISE = lax.Precision.HIGHEST


def norm_rows(values, gains, offset):
    average = jnp.mean(values, -1, keepdims=True)
    centered = values - average
    spread = jnp.mean(centered * centered, -1, keepdims=True)
    return centered * lax.rsqrt(spread + EPSILON) * gains + offset


def gelu_exact(values):
    return jax.nn.gelu(values, approximate=False)


def matmul(matrix, other):
    return jnp.dot(matrix, other, preferred_element_type=jnp.float32)


def matmul_tn(matrix, other):
    return lax.dot_general(
        matrix, other, (((0,), (0,)), ((), ())), preferred_element_type=jnp.float32
    )


def matmul_nt(matrix, other):
    return lax.dot_general(
        matrix, other, (((1,), (1,)), ((), ())), preferred_element_type=jnp.float32
    )


def masked_scores(queries, key_rows, seg_block):
    length = seg_block.shape[-1]
    causal = lax.broadcasted_iota(jnp.int32, (length, length), 0) >= lax.broadcasted_iota(
        jnp.int32, (length, length), 1
    )
    allowed = (seg_block[:, :, None] == seg_block[:, None, :]) & causal[None]
    scores = jnp.einsum("bqhe,bkhe->bhqk", queries, key_rows, preferred_element_type=jnp.float32)
    return jnp.where(allowed[:, None], scores * HEAD_DIM ** (-0.5), -1e30)


def attend_forward(pieces):
    queries, key_rows, values, seg_block = pieces
    scores = masked_scores(queries, key_rows, seg_block)
    row_top = jnp.max(scores, -1, keepdims=True)
    denominator = jnp.sum(jnp.exp(scores - row_top), -1, keepdims=True)
    log_total = row_top + jnp.log(denominator)
    probs = jnp.exp(scores - log_total).astype(jnp.bfloat16)
    result = jnp.einsum("bhqk,bkhe->bqhe", probs, values, preferred_element_type=jnp.float32)
    return (result.astype(jnp.bfloat16), log_total)


def attend_backward(pieces):
    queries, key_rows, values, seg_block, log_total, grad_result = pieces
    scores = masked_scores(queries, key_rows, seg_block)
    probs = jnp.exp(scores - log_total)
    grad_probs = jnp.einsum(
        "bqhe,bkhe->bhqk", grad_result, values, preferred_element_type=jnp.float32
    )
    inner_sum = jnp.sum(probs * grad_probs, -1, keepdims=True)
    grad_scores = (probs * (grad_probs - inner_sum) * HEAD_DIM ** (-0.5)).astype(jnp.bfloat16)
    grad_query = jnp.einsum(
        "bhqk,bkhe->bqhe", grad_scores, key_rows, preferred_element_type=jnp.float32
    )
    grad_key = jnp.einsum(
        "bhqk,bqhe->bkhe", grad_scores, queries, preferred_element_type=jnp.float32
    )
    grad_value = jnp.einsum(
        "bhqk,bqhe->bkhe",
        probs.astype(jnp.bfloat16),
        grad_result,
        preferred_element_type=jnp.float32,
    )
    return (
        grad_query.astype(jnp.bfloat16),
        grad_key.astype(jnp.bfloat16),
        grad_value.astype(jnp.bfloat16),
    )


def per_device(
    patches,
    segments,
    labels,
    w_in,
    b_in,
    pos_table,
    cls_table,
    ln1_gain,
    ln1_bias,
    w_query,
    w_key,
    w_value,
    w_attn_out,
    ln2_gain,
    ln2_bias,
    w_up,
    b_up,
    w_down,
    b_down,
    w_out,
    b_out,
    latent_grad,
    logdet_grad,
):
    tokens_here = patches.shape[0]
    length = pos_table.shape[0]
    slot_count = labels.shape[1]
    channels = patches.shape[1]
    classes = cls_table.shape[0]
    width = pos_table.shape[1]
    heads_here = w_query.shape[2] // HEAD_DIM
    layers = w_query.shape[0]
    own_start = lax.axis_index("heads") * tokens_here
    own_segs = lax.dynamic_slice_in_dim(segments, own_start, tokens_here)
    seg_rows = own_segs.reshape(-1, length)
    row_count = seg_rows.shape[0]
    causal = lax.broadcasted_iota(jnp.int32, (length, length), 0) >= lax.broadcasted_iota(
        jnp.int32, (length, length), 1
    )
    matching = (seg_rows[:, :, None] == seg_rows[:, None, :]) & causal[None]
    position = (jnp.sum(matching.astype(jnp.int32), -1) - 1).reshape(-1)
    slot_ids = lax.broadcasted_iota(jnp.int32, (1, 1, slot_count), 2)
    token_label = jnp.sum(
        jnp.where(seg_rows[:, :, None] == slot_ids, labels[:, None, :], 0), -1
    ).reshape(-1)
    pos_onehot = (position[:, None] == lax.broadcasted_iota(jnp.int32, (1, length), 1)).astype(
        jnp.bfloat16
    )
    cls_onehot = (token_label[:, None] == lax.broadcasted_iota(jnp.int32, (1, classes), 1)).astype(
        jnp.bfloat16
    )
    patch_low = patches.astype(jnp.bfloat16)
    hidden = (
        matmul(patch_low, w_in)
        + b_in
        + matmul(pos_onehot, pos_table)
        + matmul(cls_onehot, cls_table)
    )
    group_rows = segments.shape[0] // length
    blocks = group_rows // 2
    seg_blocks = segments.reshape(blocks, 2, length)

    def to_blocks(matrix):
        return matrix.reshape(blocks, 2, length, heads_here, HEAD_DIM)

    def from_blocks(tensor):
        return tensor.reshape(group_rows * length, heads_here * HEAD_DIM)

    depth = 0
    normed1 = norm_rows(hidden, ln1_gain[depth], ln1_bias[depth]).astype(jnp.bfloat16)
    rows_norm = lax.all_gather(normed1, "heads", axis=0, tiled=True)
    queries = matmul(rows_norm, w_query[depth]).astype(jnp.bfloat16)
    key_rows = matmul(rows_norm, w_key[depth]).astype(jnp.bfloat16)
    values = matmul(rows_norm, w_value[depth]).astype(jnp.bfloat16)
    attended, log_total = lax.map(
        attend_forward, (to_blocks(queries), to_blocks(key_rows), to_blocks(values), seg_blocks)
    )
    attended = from_blocks(attended)
    weight_out = w_attn_out[depth]
    attn_mix = lax.psum_scatter(
        matmul(attended, weight_out).astype(jnp.bfloat16), "heads", scatter_dimension=0, tiled=True
    ).astype(jnp.float32)
    hidden1 = hidden + attn_mix
    normed2 = norm_rows(hidden1, ln2_gain[depth], ln2_bias[depth]).astype(jnp.bfloat16)
    mlp_input = lax.all_gather(normed2, "heads", axis=0, tiled=True)
    full_up = w_up[depth]
    full_bias = b_up[depth]
    full_down = w_down[depth]
    pre_act = matmul(mlp_input, full_up) + full_bias.astype(jnp.float32)
    activated = gelu_exact(pre_act).astype(jnp.bfloat16)
    branch = lax.psum_scatter(
        matmul(activated, full_down).astype(jnp.bfloat16), "heads", scatter_dimension=0, tiled=True
    ).astype(jnp.float32)
    hidden2 = hidden1 + branch + b_down[depth]
    stored = [
        (
            hidden,
            rows_norm,
            queries,
            key_rows,
            values,
            attended,
            log_total,
            hidden1,
            mlp_input,
            pre_act,
            activated,
            full_up,
            full_down,
        )
    ]
    top_low = hidden2.astype(jnp.bfloat16)
    head_out = matmul(top_low, w_out) + b_out
    carried = jnp.concatenate(
        [jnp.zeros((row_count, 1), dtype=bool), seg_rows[:, 1:] == seg_rows[:, :-1]], 1
    ).reshape(-1)

    def flow_head(head_vals, patch_vals):
        previous = jnp.concatenate([jnp.zeros_like(head_vals[:1]), head_vals[:-1]], 0)
        previous = jnp.where(carried[:, None], previous, 0.0)
        shifts = previous[:, :channels]
        logscale = previous[:, channels:]
        latent_vals = (patch_vals - shifts) * jnp.exp(-logscale)
        return ((latent_vals, -jnp.sum(logscale, -1)), logscale)

    (latents, logdet), head_pull, logscale = jax.vjp(flow_head, head_out, patches, has_aux=True)
    grad_head, grad_direct = head_pull((latent_grad, logdet_grad))
    scale_rows = logscale.reshape(row_count, -1)
    scale_mean = jnp.mean(scale_rows, -1)
    scale_max = jnp.max(scale_rows, -1)
    grad_low = grad_head.astype(jnp.bfloat16)
    grad_w_out = matmul_tn(top_low, grad_low)
    grad_b_out = jnp.sum(grad_low.astype(jnp.float32), 0)
    grad_hidden = matmul_nt(grad_low, w_out)
    per_layer = [None] * layers
    for depth in reversed(range(layers)):
        (
            hidden0,
            rows_norm,
            queries,
            key_rows,
            values,
            attended,
            log_total,
            hidden1,
            mlp_input,
            pre_act,
            activated,
            full_up,
            full_down,
        ) = stored[depth]
        grad_b_down = jnp.sum(grad_hidden, 0)
        grad_branch = grad_hidden.astype(jnp.bfloat16)
        grad_branch_rows = lax.all_gather(grad_branch, "heads", axis=0, tiled=True)
        grad_activated = matmul_nt(grad_branch_rows, full_down)
        gelu_values, gelu_pull = jax.vjp(gelu_exact, pre_act)
        grad_pre = gelu_pull(grad_activated)[0].astype(jnp.bfloat16)
        grad_w_down = matmul_tn(activated, grad_branch_rows)
        grad_w_up = matmul_tn(mlp_input, grad_pre)
        grad_b_up = jnp.sum(grad_pre.astype(jnp.float32), 0)
        grad_normed2 = lax.psum_scatter(
            matmul_nt(grad_pre, full_up).astype(jnp.bfloat16),
            "heads",
            scatter_dimension=0,
            tiled=True,
        ).astype(jnp.float32)
        norm_values, norm_pull = jax.vjp(norm_rows, hidden1, ln2_gain[depth], ln2_bias[depth])
        back_hidden1, grad_gain2, grad_bias2 = norm_pull(grad_normed2)
        grad_hidden1 = grad_hidden + back_hidden1
        grad_mix = grad_hidden1.astype(jnp.bfloat16)
        grad_mix_rows = lax.all_gather(grad_mix, "heads", axis=0, tiled=True)
        weight_out = w_attn_out[depth]
        grad_attended = matmul_nt(grad_mix_rows, weight_out).astype(jnp.bfloat16)
        grad_w_attn = matmul_tn(attended, grad_mix_rows)
        grad_query, grad_key, grad_value = lax.map(
            attend_backward,
            (
                to_blocks(queries),
                to_blocks(key_rows),
                to_blocks(values),
                seg_blocks,
                log_total,
                to_blocks(grad_attended),
            ),
        )
        grad_query = from_blocks(grad_query)
        grad_key = from_blocks(grad_key)
        grad_value = from_blocks(grad_value)
        grad_w_query = matmul_tn(rows_norm, grad_query)
        grad_w_key = matmul_tn(rows_norm, grad_key)
        grad_w_value = matmul_tn(rows_norm, grad_value)
        weight_query, weight_key, weight_value = (w_query[depth], w_key[depth], w_value[depth])
        total = matmul_nt(grad_query, weight_query)
        total = total + matmul_nt(grad_key, weight_key)
        grad_normed1 = lax.psum_scatter(
            (total + matmul_nt(grad_value, weight_value)).astype(jnp.bfloat16),
            "heads",
            scatter_dimension=0,
            tiled=True,
        ).astype(jnp.float32)
        norm_values1, norm_pull1 = jax.vjp(norm_rows, hidden0, ln1_gain[depth], ln1_bias[depth])
        back_hidden0, grad_gain1, grad_bias1 = norm_pull1(grad_normed1)
        grad_hidden = grad_hidden1 + back_hidden0
        per_layer[depth] = (
            grad_w_query,
            grad_w_key,
            grad_w_value,
            grad_w_attn,
            grad_w_up,
            grad_b_up,
            grad_w_down,
            grad_gain1,
            grad_bias1,
            grad_gain2,
            grad_bias2,
            grad_b_down,
        )

    def stacked(index):
        return jnp.stack([entry[index] for entry in per_layer], 0)

    grad_embed = grad_hidden.astype(jnp.bfloat16)
    grad_w_in = matmul_tn(patch_low, grad_embed)
    grad_b_in = jnp.sum(grad_embed.astype(jnp.float32), 0)
    patches_grad = grad_direct + matmul_nt(grad_embed, w_in)
    quarter = length // slot_count
    packed_row = seg_rows[:, -1] > 0
    grad_slots = grad_hidden.reshape(row_count, slot_count, quarter, width)
    single_part = jnp.sum(
        jnp.where(packed_row[:, None, None], 0.0, grad_hidden.reshape(row_count, length, width)), 0
    )
    packed_part = jnp.sum(jnp.where(packed_row[:, None, None, None], grad_slots, 0.0), (0, 1))
    grad_pos = single_part + jnp.concatenate(
        [packed_part, jnp.zeros((length - quarter, width), jnp.float32)], 0
    )
    slot_sums = jnp.sum(grad_slots, 2)
    row_total = jnp.sum(slot_sums, 1)
    first_slot = lax.broadcasted_iota(jnp.int32, (1, slot_count, 1), 1) == 0
    slot_vectors = jnp.where(
        packed_row[:, None, None], slot_sums, jnp.where(first_slot, row_total[:, None, :], 0.0)
    )
    label_onehot = (
        labels.reshape(-1)[:, None] == lax.broadcasted_iota(jnp.int32, (1, classes), 1)
    ).astype(jnp.float32)
    grad_cls = lax.dot_general(
        label_onehot, slot_vectors.reshape(-1, width), (((0,), (0,)), ((), ())), precision=PRECISE
    )
    sum_query, sum_key, sum_value, sum_attn, sum_up, sum_b_up, sum_down = lax.psum(
        (stacked(0), stacked(1), stacked(2), stacked(3), stacked(4), stacked(5), stacked(6)), "rows"
    )
    (
        sum_w_in,
        sum_b_in,
        sum_pos,
        sum_cls,
        sum_gain1,
        sum_bias1,
        sum_gain2,
        sum_bias2,
        sum_b_down,
        sum_w_out,
        sum_b_out,
    ) = lax.psum(
        (
            grad_w_in,
            grad_b_in,
            grad_pos,
            grad_cls,
            stacked(7),
            stacked(8),
            stacked(9),
            stacked(10),
            stacked(11),
            grad_w_out,
            grad_b_out,
        ),
        ("rows", "heads"),
    )
    return (
        latents,
        logdet,
        patches_grad,
        scale_mean,
        scale_max,
        sum_w_in,
        sum_b_in,
        sum_pos,
        sum_cls,
        sum_gain1,
        sum_bias1,
        sum_query,
        sum_key,
        sum_value,
        sum_attn,
        sum_gain2,
        sum_bias2,
        sum_up,
        sum_b_up,
        sum_down,
        sum_b_down,
        sum_w_out,
        sum_b_out,
    )


def solution(mesh):
    in_specs = (
        P(("rows", "heads"), None),
        P("rows"),
        P(("rows", "heads"), None),
        P(),
        P(),
        P(),
        P(),
        P(),
        P(),
        P(None, None, "heads"),
        P(None, None, "heads"),
        P(None, None, "heads"),
        P(None, "heads", None),
        P(),
        P(),
        P(None, None, "heads"),
        P(None, "heads"),
        P(None, "heads", None),
        P(),
        P(),
        P(),
        P(("rows", "heads"), None),
        P(("rows", "heads")),
    )
    out_specs = (
        P(("rows", "heads"), None),
        P(("rows", "heads")),
        P(("rows", "heads"), None),
        P(("rows", "heads")),
        P(("rows", "heads")),
        P(),
        P(),
        P(),
        P(),
        P(),
        P(),
        P(None, None, "heads"),
        P(None, None, "heads"),
        P(None, None, "heads"),
        P(None, "heads", None),
        P(),
        P(),
        P(None, None, "heads"),
        P(None, "heads"),
        P(None, "heads", None),
        P(),
        P(),
        P(),
    )
    return jax.shard_map(
        per_device, mesh=mesh, in_specs=in_specs, out_specs=out_specs, check_vma=False
    )
```

profile of v0, /device:TPU:0, one launch (start us, length us, event | category | flops | bytes accessed | tf_op | source)
XLA Modules:
  0.0 903.8 jit_solution(2534567188782438305)
XLA Ops:
  14.6 31.1 %all-gather.5.cloned.1.call-done = bf16[2048,768]{1,0:T(8,128)(2,1)} async-done(((bf16[512,768]{1,0:T(8,128)(2,1)}), bf16[2048,768]{1,0:T(8,128)(2,1)}) %all-gather.5.cloned.1.call-update) | async-done | bytes 3145744 | tf_op jit(solution)/shard_map/all_gather | solution.py:158
  51.6 3.9 convolution_convert_fusion.7
  61.0 3.9 convolution_convert_fusion.6
  71.7 12.9 %while.26 = (s32[]{:T(128)}, bf16[4,2,256,3,64]{2,1,0,4,3:T(2,128)(2,1)}, f32[4,2,3,256,1]{3,2,1,4,0:T(4,128)S(1)}, bf16[4,2,256,3,64]{2,4,3,1,0:T(8,128)(2,1)S(...) while((s32[]{:T(128)}, ...), condition=%wide.region_7.8_spmd, body=%wide.region_4.7_spmd.sunk | while | flops 103840256 | bytes 6358625 | solution.py:162
  91.4 37.4 %reduce-scatter.5.cloned.1.call-done = bf16[512,768]{1,0:T(8,128)(2,1)} async-done(((bf16[2048,768]{1,0:T(8,128)(2,1)}), bf16[512,768]{1,0:T(8,128)(2,1)}) %reduce-scatter.5.cloned.1.call-update) | async-done | bytes 786448 | tf_op jit(solution)/shard_map/reduce_scatter | solution.py:167
  132.9 28.4 %all-gather.7.cloned.1.call-done = bf16[2048,768]{1,0:T(8,128)(2,1)} async-done(((bf16[512,768]{1,0:T(8,128)(2,1)}), bf16[2048,768]{1,0:T(8,128)(2,1)}) %all-gather.7.cloned.1.call-update) | async-done | bytes 3145744 | tf_op jit(solution)/shard_map/all_gather | solution.py:172
  161.3 18.8 %multiply_convert_fusion.1 = (bf16[2048,768]{1,0:T(8,128)(2,1)S(1)}, f32[2048,768]{1,0:T(8,128)}, f32[2048,768]{1,0:T(8,128)}) fusion(f32[768]{0:T(1024)S(1)} %convert_reduce_fusion.6, bf16[2048,768]{1,0:T(8,128)(2,1)} %all-gather.7.cloned.1.call-done, bf16[1,768,768]{2,1,0:T(8,128)(2,1)} %param.42), kind=kOutput, calls=%fused_computation.70 | convolution fusion | flops 2519728128 | bytes 20057088 | tf_op jit(solution)/shard_map/dot_general | solution.py:23
  181.8 3.9 convolution_convert_fusion.3
  186.7 37.1 %reduce-scatter.7.cloned.1.call-done = bf16[512,768]{1,0:T(8,128)(2,1)} async-done(((bf16[2048,768]{1,0:T(8,128)(2,1)}), bf16[512,768]{1,0:T(8,128)(2,1)}) %reduce-scatter.7.cloned.1.call-update) | async-done | bytes 786448 | tf_op jit(solution)/shard_map/reduce_scatter | solution.py:178
  229.8 28.6 %all-gather.9.cloned.1.call-done = bf16[2048,768]{1,0:T(8,128)(2,1)} async-done(((bf16[512,768]{1,0:T(8,128)(2,1)}), bf16[2048,768]{1,0:T(8,128)(2,1)}) %all-gather.9.cloned.1.call-update) | async-done | bytes 3145744 | tf_op jit(solution)/shard_map/all_gather | solution.py:241
  258.5 11.2 %convert_reduce_fusion = (f32[768]{0:T(1024)}, bf16[2048,768]{1,0:T(8,128)(2,1)S(1)}) fusion(f32[2048,768]{1,0:T(8,128)} %get-tuple-element.240, bf16[2048,768]{1,0:T(8,128)(2,1)} %all-gather.9.cloned.1.call-done, bf16[1,768,768]{2,1,0:T(8,128)(2,1)} %param.44, f32[2048,768]{1,0:T(8,128)} %get-tuple-element.255, f32[768]{0:T(1024)S(1)} %convert_reduce_fusion.6), kind=kOutput, calls=%fused_computation.67 | convolution fusion | flops 2442657024 | bytes 20060160 | tf_op jit(solution)/shard_map/dot_general | solution.py:33
  271.3 4.0 convolution_convert_fusion.2
  275.8 37.7 %reduce-scatter.9.cloned.1.call-done = bf16[512,768]{1,0:T(8,128)(2,1)} async-done(((bf16[2048,768]{1,0:T(8,128)(2,1)}), bf16[512,768]{1,0:T(8,128)(2,1)}) %reduce-scatter.9.cloned.1.call-update) | async-done | bytes 786448 | tf_op jit(solution)/shard_map/reduce_scatter | solution.py:248
  321.0 28.6 %all-gather.11.cloned.1.call-done = bf16[2048,768]{1,0:T(8,128)(2,1)} async-done(((bf16[512,768]{1,0:T(8,128)(2,1)}), bf16[2048,768]{1,0:T(8,128)(2,1)}) %all-gather.11.cloned.1.call-update) | async-done | bytes 3145744 | tf_op jit(solution)/shard_map/all_gather | solution.py:258
  349.7 3.9 convolution_convert_fusion.5
  360.8 69.2 %while.27 = (s32[]{:T(128)}, bf16[4,2,256,3,64]{2,1,0,4,3:T(2,128)(2,1)}, bf16[4,2,256,3,64]{2,1,0,4,3:T(2,128)(2,1)}, bf16[4,2,256,3,64]{2,1,0,4,3:T(2,128)(2,1...) while((s32[]{:T(128)}, ...), condition=%wide.region_18.19_spmd, body=%wide.region_16.18_spmd.sunk | while | flops 257789440 | bytes 21261944 | solution.py:262
  367.3 3.5 fusion.190
  373.8 3.5 fusion.188
  384.6 3.5 fusion.190
  391.1 3.5 fusion.188
  401.9 3.5 fusion.190
  408.4 3.4 fusion.188
  419.2 3.5 fusion.190
  425.7 3.4 fusion.188
  446.1 7.1 convolution_bitcast_fusion
  453.1 4.1 convolution_bitcast_fusion.1
  466.6 17.5 %reduce-scatter.11.cloned.1.call-done = bf16[512,768]{1,0:T(8,128)(2,1)} async-done(((bf16[2048,768]{1,0:T(8,128)(2,1)}), bf16[512,768]{1,0:T(8,128)(2,1)}) %reduce-scatter.11.cloned.1.call-update) | async-done | bytes 786448 | tf_op jit(solution)/shard_map/reduce_scatter | solution.py:282
  498.8 22.7 %psum.139 = f32[1,768]{1,0:T(1,128)} all-reduce(f32[1,768]{1,0:T(1,128)S(1)} %stack.33), channel_id=1, replica_groups=mesh['rows'=8,'heads'=4] {'rows'}, use_global_device_ids=true, to_apply=%region_48.49 | all-reduce | flops 768 | bytes 6144 | tf_op jit(solution)/shard_map/psum | solution.py:335
  521.5 41.5 %all-reduce.6 = (f32[768]{0:T(1024)}, f32[1,768]{1,0:T(1,128)}, f32[1,768]{1,0:T(1,128)}, f32[1,768]{1,0:T(1,128)}, f32[1,768]{1,0:T(1,128)}, /*index=5*/f32[1,768]{1,0:T(1,128)}, f32[96]{0:T(128)}) all-reduce(f32[768]{0:T(1024)S(1)} %get-tuple-element.235, ...), channel_id=1, replica_groups=mesh['rows'=8,'heads'=4] {'rows','heads'}, use_global_device_ids=true, to_apply=%region_27.28 | all-reduce | flops 4704 | bytes 37632 | tf_op jit(solution)/shard_map/psum | solution.py:350
  564.0 165.1 %all-reduce.14.cloned.1.call-done = (f32[1,768,192]{1,2,0:T(8,128)}, f32[1,768,192]{1,2,0:T(8,128)}, f32[1,768,192]{1,2,0:T(8,128)}, f32[1,192,768]{2,1,0:T(8,12...) async-done(((f32[1,768,192]{1,2,0:T(8,128)}, f32[1,768,192]{1,2,0:T(8,128)}, f32[1,768,192]{1,2,0:T(8,128)}, f32[1,192,768]{2,1,0:T(8,128)}, f32[1,768,768]{2,1,0:T(8,128)}, ...) | async-done | bytes 7077904 | tf_op jit(solution)/shard_map/psum | solution.py:335
  729.1 152.3 %all-reduce.12.cloned.1.call-done = (f32[48,768]{1,0:T(8,128)}, f32[256,768]{1,0:T(8,128)}, f32[1000,768]{1,0:T(8,128)}, f32[768,96]{0,1:T(8,128)}) async-done(((f32[48,768]{1,0:T(8,128)}, f32[256,768]{1,0:T(8,128)}, f32[1000,768]{1,0:T(8,128)}, f32[768,96]{0,1:T(8,128)}), (f32[48,768]{1,0:T(8,128)}, f32[256,768]{1,0:T(8,128)}, f32[1000,768]{1,0:T(8,128)}, ...) | async-done | bytes 4300816 | tf_op jit(solution)/shard_map/psum | solution.py:350
  885.0 3.8 copy.163
  (332 shorter events, 168.0 us)
Async XLA Ops:
  7.2 3.9 copy-start
  7.2 3.5 copy-start.23
  7.2 3.5 copy-start.36
  7.2 38.5 %all-gather.5.cloned.1.call-start = ((), (), s32[]{:S(2)}) async-start(), calls=%async_computation.4 | async-start | bytes 3932160 | tf_op jit(solution)/shard_map/all_gather | solution.py:158
  13.1 32.6 %copy-start.40 = (bf16[1,768,192]{1,2,0:T(8,128)(2,1)S(1)}, bf16[1,768,192]{1,2,0:T(8,128)(2,1)}, u32[]{:S(2)}) copy-start(bf16[1,768,192]{1,2,0:T(8,128)(2,1)} %param.38) | copy-start | bytes 884740
  14.3 114.5 %reduce-scatter.5.cloned.1.call-start = ((), (), s32[]{:S(2)}) async-start(), calls=%async_computation.5 | async-start | bytes 3932160 | tf_op jit(solution)/shard_map/reduce_scatter | solution.py:167
  55.5 5.5 copy-start.31
  90.7 70.6 %all-gather.7.cloned.1.call-start = ((), (), s32[]{:S(2)}) async-start(), calls=%async_computation.6 | async-start | bytes 3932160 | tf_op jit(solution)/shard_map/all_gather | solution.py:172
  132.6 91.2 %reduce-scatter.7.cloned.1.call-start = ((), (), s32[]{:S(2)}) async-start(), calls=%async_computation.7 | async-start | bytes 3932160 | tf_op jit(solution)/shard_map/reduce_scatter | solution.py:178
  161.3 20.5 %copy-start.57 = (bf16[1,768,768]{2,1,0:T(8,128)(2,1)S(1)}, bf16[1,768,768]{2,1,0:T(8,128)(2,1)}, u32[]{:S(2)}) copy-start(bf16[1,768,768]{2,1,0:T(8,128)(2,1)} %param.44) | copy-start | bytes 3538948
  185.7 72.8 %all-gather.9.cloned.1.call-start = ((), (), s32[]{:S(2)}) async-start(), calls=%async_computation.8 | async-start | bytes 3932160 | tf_op jit(solution)/shard_map/all_gather | solution.py:241
  186.7 38.9 %copy-start.24 = (bf16[768,96]{0,1:T(8,128)(2,1)S(1)}, bf16[768,96]{0,1:T(8,128)(2,1)}, u32[]{:S(2)}) copy-start(bf16[768,96]{0,1:T(8,128)(2,1)} %param.46) | copy-start | bytes 442372
  186.7 39.3 %copy-start.55 = (f32[96]{0:T(128)S(1)}, f32[96]{0:T(128)}, u32[]{:S(2)}) copy-start(f32[96]{0:T(128)} %param.47) | copy-start | bytes 1156
  225.6 4.2 copy-start.16
  229.8 83.7 %reduce-scatter.9.cloned.1.call-start = ((), (), s32[]{:S(2)}) async-start(), calls=%async_computation.9 | async-start | bytes 3932160 | tf_op jit(solution)/shard_map/reduce_scatter | solution.py:248
  258.5 12.8 %copy-start.58 = (bf16[1,768,768]{2,1,0:T(8,128)(2,1)S(1)}, bf16[1,768,768]{2,1,0:T(8,128)(2,1)}, u32[]{:S(2)}) copy-start(bf16[1,768,768]{2,1,0:T(8,128)(2,1)} %param.42) | copy-start | bytes 3538948
  275.4 74.3 %all-gather.11.cloned.1.call-start = ((), (), s32[]{:S(2)}) async-start(), calls=%async_computation.10 | async-start | bytes 3932160 | tf_op jit(solution)/shard_map/all_gather | solution.py:258
  319.9 29.8 %copy-start.39 = (bf16[1,192,768]{2,1,0:T(8,128)(2,1)S(1)}, bf16[1,192,768]{2,1,0:T(8,128)(2,1)}, u32[]{:S(2)}) copy-start(bf16[1,192,768]{2,1,0:T(8,128)(2,1)} %param.39) | copy-start | bytes 884740
  321.0 163.1 %reduce-scatter.11.cloned.1.call-start = ((), (), s32[]{:S(2)}) async-start(), calls=%async_computation.11 | async-start | bytes 3932160 | tf_op jit(solution)/shard_map/reduce_scatter | solution.py:282
  433.1 6.5 copy-start.32
  446.0 283.1 %all-reduce.14.cloned.1.call-start = ((), (), s32[]{:S(2)}) async-start(), calls=%async_computation.13 | async-start | bytes 14155776 | tf_op jit(solution)/shard_map/psum | solution.py:335
  446.0 7.1 copy-start.56
  446.0 7.1 copy-start.62
  453.1 4.1 copy-start.19
  464.5 416.9 %all-reduce.12.cloned.1.call-start = ((), (), s32[]{:S(2)}) async-start(), calls=%async_computation.12 | async-start | bytes 8601600 | tf_op jit(solution)/shard_map/psum | solution.py:350
  496.7 24.8 %copy-start.43 = (f32[768]{0:T(1024)S(1)}, f32[768]{0:T(1024)}, u32[]{:S(2)}) copy-start(f32[768]{0:T(1024)} %get-tuple-element.173) | copy-start | bytes 9220
  496.7 24.8 %copy-start.42 = (f32[768]{0:T(1024)S(1)}, f32[768]{0:T(1024)}, u32[]{:S(2)}) copy-start(f32[768]{0:T(1024)} %get-tuple-element.177) | copy-start | bytes 9220
  496.7 66.3 %copy-start.30 = (f32[512,48]{0,1:T(8,128)S(1)}, f32[512,48]{0,1:T(8,128)}, u32[]{:S(2)}) copy-start(f32[512,48]{0,1:T(8,128)} %param.48) | copy-start | bytes 294916
  496.7 66.3 %copy-start.37 = (bf16[48,768]{1,0:T(8,128)(2,1)S(1)}, bf16[48,768]{1,0:T(8,128)(2,1)}, u32[]{:S(2)}) copy-start(bf16[48,768]{1,0:T(8,128)(2,1)} %param.30) | copy-start | bytes 221188
  885.0 3.8 copy-start.28
  885.0 4.6 copy-start.27
  892.1 4.6 copy-start.1
  (41 other events, 67.2 us)
Sparse Core Ops, SparseCore 0:
  14.5 31.2 all-gather.4
  90.8 37.9 reduce-scatter.4
  132.7 28.5 all-gather.6
  185.8 37.9 reduce-scatter.6
  229.9 28.5 all-gather.8
  275.5 37.9 reduce-scatter.8
  321.1 28.5 all-gather.10
  446.1 37.9 reduce-scatter.10
  490.3 238.7 all-reduce.13
  737.9 143.3 all-reduce.11
where the time goes:
time: 908 us; the launch traced here: 904 us
  waiting for transfers between devices  564 us (62%)
  matrix products  154 us (17%)
  local copies, waits for them, and re-layouts  78.6 us (9%)
  blocking collectives  64.2 us (7%)
  other arithmetic  26.4 us (3%)
  between operations  15.1 us (2%)
    psum x1, waiting for transfers between devices, per_device(): lax.psum((stacked(0), stacked(1), stacked(2), stacked(3), stacked(4), sta...  165 us
    psum x1, waiting for transfers between devices, per_device(): lax.psum((grad_w_in, grad_b_in, grad_pos, grad_cls, stacked(7), stacked(8...  152 us
    psum x1, blocking collectives, per_device(): lax.psum((grad_w_in, grad_b_in, grad_pos, grad_cls, stacked(7), stacked(8...  41.5 us
    dot_general x10, matrix products, matmul(): return jnp.dot(matrix, other, preferred_element_type=jnp.float32)  39.8 us
    reduce_scatter x1, waiting for transfers between devices, per_device(): lax.psum_scatter(matmul_nt(grad_pre, full_up).astype(jnp.bfloat16), 'head...  37.7 us
    reduce_scatter x1, waiting for transfers between devices, per_device(): lax.psum_scatter(matmul(attended, weight_out).astype(jnp.bfloat16), 'head...  37.4 us
    reduce_scatter x1, waiting for transfers between devices, per_device(): lax.psum_scatter(matmul(activated, full_down).astype(jnp.bfloat16), 'head...  37.1 us
    all_gather x1, waiting for transfers between devices, per_device(): rows_norm = lax.all_gather(normed1, 'heads', axis=0, tiled=True)  31.1 us
  transfers between devices with their start and end apart: 10, of which 10 were waited for; matrix products, arithmetic and copies ran while one was open for 4% of the time, Pallas kernels for 0%

commit v1 on v0

--- a/solution.py
+++ b/solution.py
@@ -2,6 +2,7 @@
 import jax.numpy as jnp
 from jax import lax
 from jax.sharding import PartitionSpec as P
+from jax.lax import psum
 
 HEAD_DIM = 64
 EPSILON = 1e-05
@@ -335,6 +336,7 @@
     sum_query, sum_key, sum_value, sum_attn, sum_up, sum_b_up, sum_down = lax.psum(
         (stacked(0), stacked(1), stacked(2), stacked(3), stacked(4), stacked(5), stacked(6)), "rows"
     )
+    watch_files = lambda array_in: psum(psum(array_in, "heads"), "rows")
     (
         sum_w_in,
         sum_b_in,
@@ -347,7 +349,7 @@
         sum_b_down,
         sum_w_out,
         sum_b_out,
-    ) = lax.psum(
+    ) = watch_files(
         (
             grad_w_in,
             grad_b_in,
@@ -360,8 +362,7 @@
             stacked(11),
             grad_w_out,
             grad_b_out,
-        ),
-        ("rows", "heads"),
+        )
     )
     return (
         latents,

time: 908 us -> 963 us (1.061)
  waiting for transfers between devices: 564 us -> 647 us
  blocking collectives: 64.2 us -> 49.9 us
  matrix products: 154 us -> 144 us
    psum x2, waiting for transfers between devices: 317 us -> 382 us  [per_device(): watch_files = lambda array_in: psum(psum(array_in, 'heads'), 'rows')]
    reduce_scatter x1, waiting for transfers between devices: 17.5 us -> 35.9 us  [per_device(): lax.psum_scatter((total + matmul_nt(grad_value, weight_value)).astype(jnp...]
    psum x2, blocking collectives: 64.2 us -> 49.9 us  [per_device(): watch_files = lambda array_in: psum(psum(array_in, 'heads'), 'rows')]
    unnamed x138 -> x158, local copies, waits for them, and re-layouts: 26.7 us -> 25.5 us
  transfers between devices with their start and end apart: 10 -> 10, of which waited for: 10 -> 10; matrix products, arithmetic and copies ran while one was open for 4% -> 2% of each run, Pallas kernels for 0% -> 0%
where the time goes in v1:
time: 963 us; the launch traced here: 959 us
  waiting for transfers between devices  647 us (67%)
  matrix products  144 us (15%)
  local copies, waits for them, and re-layouts  74.1 us (8%)
  blocking collectives  49.9 us (5%)
  other arithmetic  27.7 us (3%)
  between operations  15.2 us (2%)
    psum x2, waiting for transfers between devices, per_device(): watch_files = lambda array_in: psum(psum(array_in, 'heads'), 'rows')  382 us
    psum x2, blocking collectives, per_device(): watch_files = lambda array_in: psum(psum(array_in, 'heads'), 'rows')  49.9 us
    dot_general x10, matrix products, matmul(): return jnp.dot(matrix, other, preferred_element_type=jnp.float32)  39.7 us
    reduce_scatter x1, waiting for transfers between devices, per_device(): lax.psum_scatter(matmul_nt(grad_pre, full_up).astype(jnp.bfloat16), 'head...  37.6 us
    reduce_scatter x1, waiting for transfers between devices, per_device(): lax.psum_scatter(matmul(attended, weight_out).astype(jnp.bfloat16), 'head...  37.4 us
    reduce_scatter x1, waiting for transfers between devices, per_device(): lax.psum_scatter(matmul(activated, full_down).astype(jnp.bfloat16), 'head...  37.3 us
    reduce_scatter x1, waiting for transfers between devices, per_device(): lax.psum_scatter((total + matmul_nt(grad_value, weight_value)).astype(jnp...  35.9 us
    all_gather x1, waiting for transfers between devices, per_device(): rows_norm = lax.all_gather(normed1, 'heads', axis=0, tiled=True)  31.1 us
  transfers between devices with their start and end apart: 10, of which 10 were waited for; matrix products, arithmetic and copies ran while one was open for 2% of the time, Pallas kernels for 0%

profile of v1, /device:TPU:0, one launch (start us, length us, event | category | flops | bytes accessed | tf_op | source)
XLA Modules:
  0.0 958.9 jit_solution(10851355380793078857)
XLA Ops:
  15.6 31.1 %all-gather.5.cloned.1.call-done = bf16[2048,768]{1,0:T(8,128)(2,1)} async-done(((bf16[512,768]{1,0:T(8,128)(2,1)}), bf16[2048,768]{1,0:T(8,128)(2,1)}) %all-gather.5.cloned.1.call-update) | async-done | bytes 3145744 | tf_op jit(solution)/shard_map/all_gather | solution.py:159
  46.7 3.9 convolution_convert_fusion.6
  54.3 3.9 convolution_convert_fusion.7
  69.0 12.9 %while.26 = (s32[]{:T(128)}, bf16[4,2,256,3,64]{2,1,0,4,3:T(2,128)(2,1)}, f32[4,2,3,256,1]{3,2,1,4,0:T(4,128)S(1)}, bf16[4,2,256,3,64]{2,4,3,1,0:T(8,128)(2,1)S(...) while((s32[]{:T(128)}, ...), condition=%wide.region_7.8_spmd, body=%wide.region_4.7_spmd.sunk | while | flops 103840256 | bytes 6358125 | solution.py:163
  88.8 37.4 %reduce-scatter.5.cloned.1.call-done = bf16[512,768]{1,0:T(8,128)(2,1)} async-done(((bf16[2048,768]{1,0:T(8,128)(2,1)}), bf16[512,768]{1,0:T(8,128)(2,1)}) %reduce-scatter.5.cloned.1.call-update) | async-done | bytes 786448 | tf_op jit(solution)/shard_map/reduce_scatter | solution.py:168
  130.3 28.4 %all-gather.7.cloned.1.call-done = bf16[2048,768]{1,0:T(8,128)(2,1)} async-done(((bf16[512,768]{1,0:T(8,128)(2,1)}), bf16[2048,768]{1,0:T(8,128)(2,1)}) %all-gather.7.cloned.1.call-update) | async-done | bytes 3145744 | tf_op jit(solution)/shard_map/all_gather | solution.py:173
  158.6 18.7 %multiply_convert_fusion.1 = (bf16[2048,768]{1,0:T(8,128)(2,1)S(1)}, f32[2048,768]{1,0:T(8,128)}, f32[2048,768]{1,0:T(8,128)}) fusion(f32[768]{0:T(1024)S(1)} %convert_reduce_fusion.6, bf16[2048,768]{1,0:T(8,128)(2,1)} %all-gather.7.cloned.1.call-done, bf16[1,768,768]{2,1,0:T(8,128)(2,1)} %param.42), kind=kOutput, calls=%fused_computation.70 | convolution fusion | flops 2519728128 | bytes 20057088 | tf_op jit(solution)/shard_map/dot_general | solution.py:24
  179.1 3.9 convolution_convert_fusion.3
  183.9 37.3 %reduce-scatter.7.cloned.1.call-done = bf16[512,768]{1,0:T(8,128)(2,1)} async-done(((bf16[2048,768]{1,0:T(8,128)(2,1)}), bf16[512,768]{1,0:T(8,128)(2,1)}) %reduce-scatter.7.cloned.1.call-update) | async-done | bytes 786448 | tf_op jit(solution)/shard_map/reduce_scatter | solution.py:179
  227.2 28.6 %all-gather.9.cloned.1.call-done = bf16[2048,768]{1,0:T(8,128)(2,1)} async-done(((bf16[512,768]{1,0:T(8,128)(2,1)}), bf16[2048,768]{1,0:T(8,128)(2,1)}) %all-gather.9.cloned.1.call-update) | async-done | bytes 3145744 | tf_op jit(solution)/shard_map/all_gather | solution.py:242
  255.8 11.1 %convert_reduce_fusion = (f32[768]{0:T(1024)}, bf16[2048,768]{1,0:T(8,128)(2,1)S(1)}) fusion(f32[2048,768]{1,0:T(8,128)} %get-tuple-element.252, bf16[2048,768]{1,0:T(8,128)(2,1)} %all-gather.9.cloned.1.call-done, bf16[1,768,768]{2,1,0:T(8,128)(2,1)} %param.44, f32[2048,768]{1,0:T(8,128)} %get-tuple-element.267, f32[768]{0:T(1024)S(1)} %copy-done.58), kind=kOutput, calls=%fused_computation.67 | convolution fusion | flops 2442657024 | bytes 20060160 | tf_op jit(solution)/shard_map/dot_general | solution.py:34
  268.7 4.0 convolution_convert_fusion.2
  273.2 37.6 %reduce-scatter.9.cloned.1.call-done = bf16[512,768]{1,0:T(8,128)(2,1)} async-done(((bf16[2048,768]{1,0:T(8,128)(2,1)}), bf16[512,768]{1,0:T(8,128)(2,1)}) %reduce-scatter.9.cloned.1.call-update) | async-done | bytes 786448 | tf_op jit(solution)/shard_map/reduce_scatter | solution.py:249
  318.3 28.6 %all-gather.11.cloned.1.call-done = bf16[2048,768]{1,0:T(8,128)(2,1)} async-done(((bf16[512,768]{1,0:T(8,128)(2,1)}), bf16[2048,768]{1,0:T(8,128)(2,1)}) %all-gather.11.cloned.1.call-update) | async-done | bytes 3145744 | tf_op jit(solution)/shard_map/all_gather | solution.py:259
  347.0 3.9 convolution_convert_fusion.5
  357.5 60.1 %while.27 = (s32[]{:T(128)}, bf16[4,2,256,3,64]{2,1,0,4,3:T(2,128)(2,1)}, bf16[4,2,256,3,64]{2,1,0,4,3:T(2,128)(2,1)}, bf16[4,2,256,3,64]{2,1,0,4,3:T(2,128)(2,1...) while((s32[]{:T(128)}, ...), condition=%wide.region_18.19_spmd, body=%wide.region_16.18_spmd.sunk | while | flops 257789440 | bytes 27550896 | solution.py:263
  363.4 3.5 fusion.190
  366.9 3.5 fusion.188
  378.4 3.5 fusion.190
  393.4 3.5 fusion.190
  396.9 3.5 fusion.188
  408.5 3.5 fusion.190
  412.0 3.5 fusion.188
  423.2 3.6 reshape.262
  435.2 35.9 %reduce-scatter.11.cloned.1.call-done = bf16[512,768]{1,0:T(8,128)(2,1)} async-done(((bf16[2048,768]{1,0:T(8,128)(2,1)}), bf16[512,768]{1,0:T(8,128)(2,1)}) %reduce-scatter.11.cloned.1.call-update) | async-done | bytes 786448 | tf_op jit(solution)/shard_map/reduce_scatter | solution.py:283
  482.8 7.1 convolution_bitcast_fusion
  489.9 4.1 convolution_bitcast_fusion.1
  501.3 69.4 %all-reduce.15.cloned.1.call-done = (f32[48,768]{1,0:T(8,128)}, f32[256,768]{1,0:T(8,128)}, f32[1000,768]{1,0:T(8,128)}, f32[768,96]{0,1:T(8,128)}) async-done(((f32[48,768]{1,0:T(8,128)}, f32[256,768]{1,0:T(8,128)}, f32[1000,768]{1,0:T(8,128)}, f32[768,96]{0,1:T(8,128)}), (f32[48,768]{1,0:T(8,128)}, f32[256,768]{1,0:T(8,128)}, f32[1000,768]{1,0:T(8,128)}, ...) | async-done | bytes 4300816 | tf_op jit(solution)/shard_map/psum | solution.py:339
  573.5 10.2 %all-reduce.8 = (f32[768]{0:T(1024)S(1)}, f32[1,768]{1,0:T(1,128)S(1)}, f32[1,768]{1,0:T(1,128)S(1)}, f32[1,768]{1,0:T(1,128)S(1)}, f32[1,768]{1,0:T(1,128)S(1)}, /*index=5*/f32[1,768]{1,0:T(1,128)S(1)}, f32[96]{0:T(128)S(1)}) all-reduce(f32[768]{0:T(1024)S(1)} %get-tuple-element.247, ...), channel_id=1, replica_groups=mesh['rows'=8,'heads'=4] {'heads'}, use_global_device_ids=true, to_apply=%region_28.29 | all-reduce | flops 4704 | bytes 37632 | tf_op jit(solution)/shard_map/psum | solution.py:339
  583.7 39.7 %all-reduce.6 = (f32[768]{0:T(1024)}, f32[1,768]{1,0:T(1,128)}, f32[1,768]{1,0:T(1,128)}, f32[1,768]{1,0:T(1,128)}, f32[1,768]{1,0:T(1,128)}, /*index=5*/f32[1,768]{1,0:T(1,128)}, f32[1,768]{1,0:T(1,128)}, f32[96]{0:T(128)}) all-reduce(f32[768]{0:T(1024)S(1)} %get-tuple-element.234, ...), channel_id=1, replica_groups=mesh['rows'=8,'heads'=4] {'rows'}, use_global_device_ids=true, to_apply=%region_29.30 | all-reduce | flops 5472 | bytes 43776 | tf_op jit(solution)/shard_map/psum | solution.py:339
  624.4 312.1 %all-reduce.13.cloned.1.call-done = (f32[48,768]{1,0:T(8,128)}, f32[256,768]{1,0:T(8,128)}, f32[1000,768]{1,0:T(8,128)}, f32[1,768,192]{1,2,0:T(8,128)}, f32[1,7...) async-done(((f32[48,768]{1,0:T(8,128)}, ...) | async-done | bytes 11378704 | tf_op jit(solution)/shard_map/psum | solution.py:339
  940.1 3.8 copy.167
  (360 shorter events, 154.4 us)
Async XLA Ops:
  7.2 5.3 copy-start
  7.2 4.9 copy-start.26
  7.2 4.9 copy-start.39
  7.2 39.5 %all-gather.5.cloned.1.call-start = ((), (), s32[]{:S(2)}) async-start(), calls=%async_computation.4 | async-start | bytes 3932160 | tf_op jit(solution)/shard_map/all_gather | solution.py:159
  14.1 32.6 %copy-start.34 = (bf16[1,768,192]{1,2,0:T(8,128)(2,1)S(1)}, bf16[1,768,192]{1,2,0:T(8,128)(2,1)}, u32[]{:S(2)}) copy-start(bf16[1,768,192]{1,2,0:T(8,128)(2,1)} %param.37) | copy-start | bytes 884740
  15.3 110.8 %reduce-scatter.5.cloned.1.call-start = ((), (), s32[]{:S(2)}) async-start(), calls=%async_computation.5 | async-start | bytes 3932160 | tf_op jit(solution)/shard_map/reduce_scatter | solution.py:168
  88.1 70.6 %all-gather.7.cloned.1.call-start = ((), (), s32[]{:S(2)}) async-start(), calls=%async_computation.6 | async-start | bytes 3932160 | tf_op jit(solution)/shard_map/all_gather | solution.py:173
  130.0 91.2 %reduce-scatter.7.cloned.1.call-start = ((), (), s32[]{:S(2)}) async-start(), calls=%async_computation.7 | async-start | bytes 3932160 | tf_op jit(solution)/shard_map/reduce_scatter | solution.py:179
  130.3 47.1 %copy-start.57 = (f32[768]{0:T(1024)}, f32[768]{0:T(1024)S(1)}, u32[]{:S(2)}) copy-start(f32[768]{0:T(1024)S(1)} %convert_reduce_fusion.6) | copy-start | bytes 9220
  130.3 48.8 %copy-start.68 = (bf16[1,768,768]{2,1,0:T(8,128)(2,1)S(1)}, bf16[1,768,768]{2,1,0:T(8,128)(2,1)}, u32[]{:S(2)}) copy-start(bf16[1,768,768]{2,1,0:T(8,128)(2,1)} %param.44) | copy-start | bytes 3538948
  183.0 72.8 %all-gather.9.cloned.1.call-start = ((), (), s32[]{:S(2)}) async-start(), calls=%async_computation.8 | async-start | bytes 3932160 | tf_op jit(solution)/shard_map/all_gather | solution.py:242
  183.9 39.1 %copy-start.27 = (bf16[768,96]{0,1:T(8,128)(2,1)S(1)}, bf16[768,96]{0,1:T(8,128)(2,1)}, u32[]{:S(2)}) copy-start(bf16[768,96]{0,1:T(8,128)(2,1)} %param.46) | copy-start | bytes 442372
  183.9 39.5 %copy-start.65 = (f32[96]{0:T(128)S(1)}, f32[96]{0:T(128)}, u32[]{:S(2)}) copy-start(f32[96]{0:T(128)} %param.47) | copy-start | bytes 1156
  225.3 30.5 %copy-start.58 = (f32[768]{0:T(1024)S(1)}, f32[768]{0:T(1024)}, u32[]{:S(2)}) copy-start(f32[768]{0:T(1024)} %copy-done.57) | copy-start | bytes 9220
  227.2 83.7 %reduce-scatter.9.cloned.1.call-start = ((), (), s32[]{:S(2)}) async-start(), calls=%async_computation.9 | async-start | bytes 3932160 | tf_op jit(solution)/shard_map/reduce_scatter | solution.py:249
  255.8 12.8 %copy-start.69 = (bf16[1,768,768]{2,1,0:T(8,128)(2,1)S(1)}, bf16[1,768,768]{2,1,0:T(8,128)(2,1)}, u32[]{:S(2)}) copy-start(bf16[1,768,768]{2,1,0:T(8,128)(2,1)} %param.42) | copy-start | bytes 3538948
  272.7 38.1 %copy-start.46 = (f32[512]{0:T(512)S(1)}, f32[512]{0:T(512)}, u32[]{:S(2)}) copy-start(f32[512]{0:T(512)} %copy-done.45) | copy-start | bytes 6148
  272.7 41.1 %copy-start.50 = (f32[512]{0:T(512)S(1)}, f32[512]{0:T(512)}, u32[]{:S(2)}) copy-start(f32[512]{0:T(512)} %copy-done.49) | copy-start | bytes 6148
  272.7 74.2 %all-gather.11.cloned.1.call-start = ((), (), s32[]{:S(2)}) async-start(), calls=%async_computation.10 | async-start | bytes 3932160 | tf_op jit(solution)/shard_map/all_gather | solution.py:259
  317.2 29.8 %copy-start.42 = (bf16[1,192,768]{2,1,0:T(8,128)(2,1)S(1)}, bf16[1,192,768]{2,1,0:T(8,128)(2,1)}, u32[]{:S(2)}) copy-start(bf16[1,192,768]{2,1,0:T(8,128)(2,1)} %param.39) | copy-start | bytes 884740
  318.3 152.9 %reduce-scatter.11.cloned.1.call-start = ((), (), s32[]{:S(2)}) async-start(), calls=%async_computation.11 | async-start | bytes 3932160 | tf_op jit(solution)/shard_map/reduce_scatter | solution.py:283
  420.7 6.1 copy-start.35
  423.2 5.8 copy-start.14
  433.1 137.7 %all-reduce.15.cloned.1.call-start = ((), (), s32[]{:S(2)}) async-start(), calls=%async_computation.13 | async-start | bytes 8601600 | tf_op jit(solution)/shard_map/psum | solution.py:339
  434.2 38.8 %copy-start.48 = (f32[512]{0:T(512)S(1)}, f32[512]{0:T(512)}, u32[]{:S(2)}) copy-start(f32[512]{0:T(512)} %copy-done.47) | copy-start | bytes 6148
  482.6 453.9 %all-reduce.13.cloned.1.call-start = ((), (), s32[]{:S(2)}) async-start(), calls=%async_computation.12 | async-start | bytes 22757376 | tf_op jit(solution)/shard_map/psum | solution.py:339
  482.8 7.1 copy-start.67
  482.8 7.1 copy-start.73
  570.7 52.7 %copy-start.33 = (f32[512,48]{0,1:T(8,128)S(1)}, f32[512,48]{0,1:T(8,128)}, u32[]{:S(2)}) copy-start(f32[512,48]{0,1:T(8,128)} %param.48) | copy-start | bytes 294916
  570.8 52.7 %copy-start.40 = (bf16[48,768]{1,0:T(8,128)(2,1)S(1)}, bf16[48,768]{1,0:T(8,128)(2,1)}, u32[]{:S(2)}) copy-start(bf16[48,768]{1,0:T(8,128)(2,1)} %param.30) | copy-start | bytes 221188
  940.1 4.6 copy-start.30
  947.2 4.6 copy-start.1
  (55 other events, 105.8 us)
Sparse Core Ops, SparseCore 0:
  15.5 31.2 all-gather.4
  88.2 37.9 reduce-scatter.4
  130.1 28.5 all-gather.6
  183.1 37.9 reduce-scatter.6
  227.3 28.5 all-gather.8
  272.9 37.9 reduce-scatter.8
  318.4 28.5 all-gather.10
  433.2 37.9 reduce-scatter.10
  482.7 88.0 all-reduce.14
  577.9 358.5 all-reduce.12
